TPU v7x, 32 devices: a whole 2x2x4 slice. The times are simulated.
32 devices in a mesh: groups: 2 (over y), span: 4 (over z), batch: 4 (over x, core).
Axes of the slice: x: 2, y: 2, z: 4, core: 2. Of those that a mesh axis runs over, the one named last changes fastest.
Arguments:
- embeddings: bfloat16 [8, 512, 768], P(('groups', 'batch'), 'span'), parts along dimension 0, may hold values from -3500 to 3500
- cluster_ids: int32 [8, 512], P(('groups', 'batch'), 'span'), parts along dimension 0, may hold values from 0 to 15, as said below
Outputs:
- nearest: float32 [8, 512], P(('groups', 'batch'), 'span'), parts along dimension 0
There are 2 independent parts, one for each index of `groups`. A program takes and returns all parts, laid end to end along the dimension named above; each array names one. Nothing has to cross between parts.
Inputs may be any that keep to these rules, and one draw needn't show every extreme that they name: `cluster_ids`: on one device at most 96 rows carry ids of one residue modulo 4; in every batch some residue has exactly 96 rows on every device of the span.
All inputs are finite; a program needn't handle non-finite values.
Results may differ from a plain program's by a relative error of at most 0.00061.
Values may be sent and summed in bfloat16 or wider, within the bound.
No kernel may reach another device: no remote copies, remote signals or barrier semaphores. Data moves between devices by JAX's collectives and lax.ppermute only.
A program may use at most 64 MiB of HBM per device.

v0:
```python
import math
import jax
import jax.numpy as jnp
from jax import lax
from jax.sharding import PartitionSpec as P


def normalize(embeddings):
    values = embeddings.astype(jnp.float32)
    inverse = lax.rsqrt(jnp.mean(values * values, axis=-1, keepdims=True) + 1e-06)
    return (values * inverse * (1.0 / math.sqrt(values.shape[-1]))).astype(jnp.bfloat16)


def pair_scores(left, right):
    return lax.dot_general(
        left, right, (((1,), (1,)), ((), ())), preferred_element_type=jnp.float32
    )


def per_device(embeddings, cluster_ids):
    normed = normalize(embeddings[0])
    member_ids = cluster_ids[0]
    row_count = normed.shape[0]
    own_index = lax.axis_index("span")
    own_rows = own_index * row_count + jnp.arange(row_count, dtype=jnp.int32)
    start_value = jnp.full((row_count,), -1.0, jnp.float32)
    piece_rows = lax.all_gather(normed, "span", axis=0, tiled=True)
    piece_ids = lax.all_gather(member_ids.astype(jnp.bfloat16), "span", axis=0, tiled=True)
    scores = pair_scores(normed, piece_rows)
    column_rows = jnp.arange(piece_rows.shape[0], dtype=jnp.int32)
    same_cluster = (member_ids[:, None] == piece_ids.astype(jnp.int32)[None, :]) & (
        own_rows[:, None] != column_rows[None, :]
    )
    nearest = jnp.maximum(start_value, jnp.max(jnp.where(same_cluster, scores, -1.0), axis=1))
    return nearest[None, :]


def solution(mesh):
    return jax.shard_map(
        per_device,
        mesh=mesh,
        in_specs=(P(("groups", "batch"), "span", None), P(("groups", "batch"), "span")),
        out_specs=P(("groups", "batch"), "span"),
        check_vma=False,
    )
```

profile of v0, /device:TPU:0, one launch (start us, length us, event | category | flops | bytes accessed | tf_op | source)
XLA Modules:
  0.0 32.1 jit_solution(1568791861424258728)
XLA Ops:
  0.0 0.0 copy-start
  0.0 1.1 %fusion.1 = f32[128]{0:T(128)S(1)} fusion(bf16[1,128,768]{2,1,0:T(8,128)(2,1)} %param.2), kind=kLoop, calls=%fused_computation.4 | loop fusion | flops 294784 | bytes 197120 | tf_op jit(solution)/shard_map/reduce_sum | solution.py:10
  1.1 0.0 copy-start.1
  1.1 0.6 %copy-done.1 = s32[1,128]{1,0:T(1,128)S(1)} copy-done((s32[1,128]{1,0:T(1,128)S(1)}, s32[1,128]{1,0:T(1,128)}, u32[]{:S(2)}) %copy-start.1) | copy-done | bytes 536
  1.8 12.6 %all-gather = bf16[4,1,128]{2,1,0:T(2,128)(2,1)S(1)} all-gather(bf16[1,1,128]{2,1,0:T(2,128)(2,1)S(1)} %convert_bitcast_fusion), channel_id=1, replica_groups=mesh['groups'=2,'span'=4,'batch'=4] {'span'}, dimensions={0}, use_global_device_ids=true | all-gather | bytes 1280 | tf_op jit(solution)/shard_map/all_gather | solution.py:28
  14.4 0.0 copy-done
  14.4 0.1 fusion.3
  14.5 16.6 %all_gather.7 = bf16[512,768]{1,0:T(8,128)(2,1)S(1)} all-gather(bf16[128,768]{1,0:T(8,128)(2,1)S(1)} %fusion.3), channel_id=1, replica_groups=mesh['groups'=2,'span'=4,'batch'=4] {'span'}, dimensions={0}, use_global_device_ids=true | all-gather | bytes 983040 | tf_op jit(solution)/shard_map/all_gather | solution.py:27
  31.1 0.5 %fusion = f32[128]{0:T(128)S(1)} fusion(bf16[128,768]{1,0:T(8,128)(2,1)S(1)} %fusion.3, bf16[512,768]{1,0:T(8,128)(2,1)S(1)} %all_gather.7, s32[128]{0:T(128)S(1)} %iota_add_fusion, s32[512]{0:T(512)S(1)} %bitcast.13, s32[128]{0:T(128)S(1)} %bitcast.14), kind=kOutput, calls=%fused_computation.1 | convolution fusion | flops 100990848 | bytes 986624 | tf_op jit(solution)/shard_map/dot_general | solution.py:15
  31.6 0.5 %maximum_bitcast_fusion = f32[1,128]{1,0:T(1,128)} fusion(f32[128]{0:T(128)S(1)} %fusion), kind=kLoop, calls=%fused_computation.9 | loop fusion | flops 128 | bytes 1024 | tf_op jit(solution)/shard_map/max;broadcast_in_dim | solution.py:34
  (4 shorter events, 0.0 us)
Async XLA Ops:
  0.0 14.4 %copy-start = (bf16[1,128,768]{2,1,0:T(8,128)(2,1)S(1)}, bf16[1,128,768]{2,1,0:T(8,128)(2,1)}, u32[]{:S(2)}) copy-start(bf16[1,128,768]{2,1,0:T(8,128)(2,1)} %param.2) | copy-start | bytes 589828
  1.1 0.7 %copy-start.1 = (s32[1,128]{1,0:T(1,128)S(1)}, s32[1,128]{1,0:T(1,128)}, u32[]{:S(2)}) copy-start(s32[1,128]{1,0:T(1,128)} %param.3) | copy-start | bytes 1540
where the time goes:
time: 32.3 us; the launch traced here: 32.1 us
  blocking collectives  29.2 us (90%)
  other arithmetic  1.77 us (5%)
  local copies, waits for them, and re-layouts  0.65 us (2%)
  matrix products  0.47 us (1%)
    all_gather x1, blocking collectives, per_device(): piece_rows = lax.all_gather(normed, 'span', axis=0, tiled=True)  16.6 us
    all_gather x1, blocking collectives, per_device(): lax.all_gather(member_ids.astype(jnp.bfloat16), 'span', axis=0, tiled=True)  12.6 us
    reduce_sum x1, other arithmetic, normalize(): jnp.mean(values * values, axis=-1, keepdims=True) + 1e-06  1.11 us

commit v1 on v0

--- a/solution.py
+++ b/solution.py
@@ -25,7 +25,12 @@
     own_rows = own_index * row_count + jnp.arange(row_count, dtype=jnp.int32)
     start_value = jnp.full((row_count,), -1.0, jnp.float32)
     piece_rows = lax.all_gather(normed, "span", axis=0, tiled=True)
-    piece_ids = lax.all_gather(member_ids.astype(jnp.bfloat16), "span", axis=0, tiled=True)
+    piece_ids = jnp.concatenate(
+        lax.all_to_all(
+            jnp.stack([member_ids.astype(jnp.bfloat16)] * lax.axis_size("span")), "span", 0, 0
+        ),
+        axis=0,
+    )
     scores = pair_scores(normed, piece_rows)
     column_rows = jnp.arange(piece_rows.shape[0], dtype=jnp.int32)
     same_cluster = (member_ids[:, None] == piece_ids.astype(jnp.int32)[None, :]) & (

time: 32.3 us -> 30.8 us (0.954)
  blocking collectives: 29.2 us -> 20.1 us
  starting transfers between devices: 0 us -> 6.35 us
  other arithmetic: 1.77 us -> 2.4 us
  local copies, waits for them, and re-layouts: 0.65 us -> 1.25 us
    all_gather x1 -> x0, blocking collectives: 12.6 us -> none  [per_device(): lax.all_gather(member_ids.astype(jnp.bfloat16), 'span', axis=0, tiled=True)]
    all_to_all x0 -> x1, starting transfers between devices: none -> 6.35 us  [per_device(): lax.all_to_all(jnp.stack([member_ids.astype(jnp.bfloat16)] * lax.axis_siz...]
    all_gather x1, blocking collectives: 16.6 us -> 20.1 us  [per_device(): piece_rows = lax.all_gather(normed, 'span', axis=0, tiled=True)]
    convert_element_type x0 -> x1, other arithmetic: none -> 0.7 us  [per_device(): member_ids.astype(jnp.bfloat16)]
    another operation x0 -> x1, local copies, waits for them, and re-layouts: none -> 0.6 us  [per_device(): jnp.stack([member_ids.astype(jnp.bfloat16)] * lax.axis_size('span'))]
  transfers between devices with their start and end apart: 0 -> 1, of which waited for: 0 -> 0; matrix products, arithmetic and copies ran while one was open for 0% -> 4% of each run, Pallas kernels for 0% -> 0%
where the time goes in v1:
time: 30.8 us; the launch traced here: 30.6 us
  blocking collectives  20.1 us (65%)
  starting transfers between devices  6.35 us (21%)
  other arithmetic  2.4 us (8%)
  local copies, waits for them, and re-layouts  1.25 us (4%)
  matrix products  0.47 us (2%)
    all_gather x1, blocking collectives, per_device(): piece_rows = lax.all_gather(normed, 'span', axis=0, tiled=True)  20.1 us
    all_to_all x1, starting transfers between devices, per_device(): lax.all_to_all(jnp.stack([member_ids.astype(jnp.bfloat16)] * lax.axis_siz...  6.35 us
    reduce_sum x1, other arithmetic, normalize(): jnp.mean(values * values, axis=-1, keepdims=True) + 1e-06  1.05 us
    convert_element_type x1, other arithmetic, per_device(): member_ids.astype(jnp.bfloat16)  0.7 us
    unnamed x4, local copies, waits for them, and re-layouts  0.65 us
  transfers between devices with their start and end apart: 1, of which 0 were waited for; matrix products, arithmetic and copies ran while one was open for 4% of the time, Pallas kernels for 0%

profile of v1, /device:TPU:0, one launch (start us, length us, event | category | flops | bytes accessed | tf_op | source)
XLA Modules:
  0.0 30.6 jit_solution(15222487123422209843)
XLA Ops:
  0.0 0.0 copy-start
  0.0 0.7 %convert_bitcast_fusion = bf16[128]{0:T(256)(128)(2,1)S(1)} fusion(s32[1,128]{1,0:T(1,128)} %param.3), kind=kLoop, calls=%fused_computation.12 | loop fusion | flops 128 | bytes 768 | tf_op jit(solution)/shard_map/convert_element_type | solution.py:30
  0.7 0.6 %stack.2 = bf16[4,1,128]{2,1,0:T(2,128)(2,1)} broadcast(bf16[128]{0:T(256)(128)(2,1)S(1)} %convert_bitcast_fusion), dimensions={2} | broadcast | bytes 1280 | tf_op jit(solution)/shard_map/stack | solution.py:30
  1.3 6.3 %all-to-all-start = ((bf16[4,1,128]{2,1,0:T(2,128)(2,1)}), bf16[4,1,128]{2,1,0:T(2,128)(2,1)S(1)}, u32[]{:S(2)}, u32[]{:S(2)}) async-start(bf16[4,1,128]{2,1,0:T(2,128)(2,1)} %stack.2), calls=%async_computation | async-start | bytes 4096 | tf_op jit(solution)/shard_map/all_to_all | solution.py:29
  7.6 1.0 %fusion.1 = f32[128]{0:T(128)S(1)} fusion(bf16[1,128,768]{2,1,0:T(8,128)(2,1)} %param.2), kind=kLoop, calls=%fused_computation.4 | loop fusion | flops 294784 | bytes 197120 | tf_op jit(solution)/shard_map/reduce_sum | solution.py:10
  8.7 0.0 copy-done
  8.7 0.1 fusion.3
  8.8 20.1 %all_gather.3 = bf16[512,768]{1,0:T(8,128)(2,1)S(1)} all-gather(bf16[128,768]{1,0:T(8,128)(2,1)S(1)} %fusion.3), channel_id=1, replica_groups=mesh['groups'=2,'span'=4,'batch'=4] {'span'}, dimensions={0}, use_global_device_ids=true | all-gather | bytes 983040 | tf_op jit(solution)/shard_map/all_gather | solution.py:27
  28.9 0.0 all-to-all-done
  28.9 0.0 copy-start.1
  28.9 0.6 %copy-done.1 = s32[1,128]{1,0:T(1,128)S(1)} copy-done((s32[1,128]{1,0:T(1,128)S(1)}, s32[1,128]{1,0:T(1,128)}, u32[]{:S(2)}) %copy-start.1) | copy-done | bytes 536
  29.6 0.5 %fusion = f32[128]{0:T(128)S(1)} fusion(bf16[128,768]{1,0:T(8,128)(2,1)S(1)} %fusion.3, bf16[512,768]{1,0:T(8,128)(2,1)S(1)} %all_gather.3, s32[128]{0:T(128)S(1)} %iota_add_fusion, s32[512]{0:T(512)S(1)} %bitcast.12, s32[128]{0:T(128)S(1)} %bitcast.13), kind=kOutput, calls=%fused_computation.1 | convolution fusion | flops 100990848 | bytes 986624 | tf_op jit(solution)/shard_map/dot_general | solution.py:15
  30.0 0.5 %maximum_bitcast_fusion = f32[1,128]{1,0:T(1,128)} fusion(f32[128]{0:T(128)S(1)} %fusion), kind=kLoop, calls=%fused_computation.9 | loop fusion | flops 128 | bytes 1024 | tf_op jit(solution)/shard_map/max;broadcast_in_dim | solution.py:39
  (3 shorter events, 0.0 us)
Async XLA Ops:
  0.0 8.7 %copy-start = (bf16[1,128,768]{2,1,0:T(8,128)(2,1)S(1)}, bf16[1,128,768]{2,1,0:T(8,128)(2,1)}, u32[]{:S(2)}) copy-start(bf16[1,128,768]{2,1,0:T(8,128)(2,1)} %param.2) | copy-start | bytes 589828
  1.3 27.6 %all-to-all-start = ((bf16[4,1,128]{2,1,0:T(2,128)(2,1)}), bf16[4,1,128]{2,1,0:T(2,128)(2,1)S(1)}, u32[]{:S(2)}, u32[]{:S(2)}) async-start(bf16[4,1,128]{2,1,0:T(2,128)(2,1)} %stack.2), calls=%async_computation | async-start | bytes 4096 | tf_op jit(solution)/shard_map/all_to_all | solution.py:29
  28.9 0.7 %copy-start.1 = (s32[1,128]{1,0:T(1,128)S(1)}, s32[1,128]{1,0:T(1,128)}, u32[]{:S(2)}) copy-start(s32[1,128]{1,0:T(1,128)} %param.3) | copy-start | bytes 1540
